TPU v7x, 32 devices: a whole 2x2x4 slice. The times are simulated.
32 devices in a mesh: dp: 8 (over z, x), tensor: 4 (over y, core).
Axes of the slice: x: 2, y: 2, z: 4, core: 2. Of those that a mesh axis runs over, the one named last changes fastest.
Arguments:
- tokens: bfloat16 [32768, 768], P(('dp', 'tensor')), may hold values from -6 to 6
- segment_ids: int32 [16, 2048], P('dp'), may hold values from 0 to 8, as said below
- memory_positions: int32 [16, 20], P('dp'), may hold values from 0 to 2047, as said below
- memory_rows: bfloat16 [20, 768], replicated, may hold values from -6 to 6
- qkv_weight: bfloat16 [768, 12, 192], P('dp', 'tensor'), may hold values from -0.21875 to 0.21875
- qv_bias: bfloat16 [12, 128], P('tensor'), may hold values from -3 to 3
- out_weight: bfloat16 [768, 12, 64], P('dp', 'tensor'), may hold values from -0.875 to 0.875
- out_bias: bfloat16 [768], replicated, may hold values from -1.75 to 1.75
- norm1_gain: bfloat16 [768], replicated, may hold values from 0.5 to 1.5
- norm1_bias: bfloat16 [768], replicated, may hold values from -1.75 to 1.75
- up_weight: bfloat16 [768, 3072], P('dp', 'tensor'), may hold values from -0.21875 to 0.21875
- up_bias: bfloat16 [3072], P('tensor'), may hold values from -3 to 3
- down_weight: bfloat16 [768, 3072], P('dp', 'tensor'), may hold values from -0.109375 to 0.109375
- down_bias: bfloat16 [768], replicated, may hold values from -1.75 to 1.75
- norm2_gain: bfloat16 [768], replicated, may hold values from 0.5 to 1.5
- norm2_bias: bfloat16 [768], replicated, may hold values from -1.75 to 1.75
- out_cotangent: bfloat16 [32768, 768], P(('dp', 'tensor')), may hold values from -6 to 6
Outputs:
- block_out: bfloat16 [32768, 768], P(('dp', 'tensor'))
- grad_tokens: float32 [32768, 768], P(('dp', 'tensor'))
- grad_memory_rows: float32 [20, 768], replicated
- grad_qkv_weight: float32 [768, 12, 192], P('dp', 'tensor')
- grad_qv_bias: float32 [12, 128], P('tensor')
- grad_out_weight: float32 [768, 12, 64], P('dp', 'tensor')
- grad_out_bias: float32 [768], replicated
- grad_norm1_gain: float32 [768], replicated
- grad_norm1_bias: float32 [768], replicated
- grad_up_weight: float32 [768, 3072], P('dp', 'tensor')
- grad_up_bias: float32 [3072], P('tensor')
- grad_down_weight: float32 [768, 3072], P('dp', 'tensor')
- grad_down_bias: float32 [768], replicated
- grad_norm2_gain: float32 [768], replicated
- grad_norm2_bias: float32 [768], replicated
Inputs may be any that keep to these rules, and one draw needn't show every extreme that they name: `segment_ids`: never falling along a group; each group begins with segment 0 of at least 512 positions and holds every segment up to 8. `memory_positions`: within a group all positions differ; read rows lie among the first 512 positions, the first at 0, write rows among the last 512, the first at 2047.
All inputs are finite; a program needn't handle non-finite values.
Results may differ from a plain program's by a relative error of at most 0.015.
Values may be sent and summed in bfloat16 or wider, within the bound.
A program may use at most 192 MiB of HBM per device.

v0:
```python
import jax
import jax.numpy as jnp
from jax import lax
from jax.sharding import PartitionSpec as P

QBLOCK = 512
EPSILON = 1e-12
MASKED = -1e30


def layer_norm(values, norm_gain, norm_shift):
    centre = values - jnp.mean(values, axis=-1, keepdims=True)
    spread = jnp.mean(centre * centre, axis=-1, keepdims=True)
    return centre * lax.rsqrt(spread + EPSILON) * norm_gain + norm_shift


def gelu_exact(values):
    return jax.nn.gelu(values, approximate=False)


def block_inputs(block_index, segments, query_all, key_all, value_all, score_scale):
    group_len = segments.shape[1]
    block_count = group_len // QBLOCK
    group_index = block_index // block_count
    within = block_index % block_count * QBLOCK
    first_row = group_index * group_len + within
    query_rows = lax.dynamic_slice_in_dim(query_all, first_row, QBLOCK, 0)
    key_rows = lax.dynamic_slice_in_dim(key_all, group_index * group_len, group_len, 0)
    value_rows = lax.dynamic_slice_in_dim(value_all, group_index * group_len, group_len, 0)
    group_segments = lax.dynamic_index_in_dim(segments, group_index, 0, keepdims=False)
    query_segments = lax.dynamic_slice_in_dim(group_segments, within, QBLOCK, 0)
    visible = (group_segments[None, :] == 0) | (group_segments[None, :] == query_segments[:, None])
    scores = (
        jnp.einsum("bhe,ghe->hbg", query_rows, key_rows, preferred_element_type=jnp.float32)
        * score_scale
    )
    scores = jnp.where(visible[None], scores, MASKED)
    return (first_row, group_index * group_len, query_rows, key_rows, value_rows, scores)


def attend_forward(query_all, key_all, value_all, segments, score_scale):
    block_total = query_all.shape[0] // QBLOCK

    def one_block(block_index):
        _, _, _, _, value_rows, scores = block_inputs(
            block_index, segments, query_all, key_all, value_all, score_scale
        )
        row_peak = jnp.max(scores, axis=-1, keepdims=True)
        exp_scores = jnp.exp(scores - row_peak)
        row_total = jnp.sum(exp_scores, axis=-1, keepdims=True)
        weights = (exp_scores / row_total).astype(jnp.bfloat16)
        head_mixed = jnp.einsum(
            "hbg,ghe->bhe", weights, value_rows, preferred_element_type=jnp.float32
        )
        return (head_mixed.astype(jnp.bfloat16), (row_peak + jnp.log(row_total))[..., 0])

    head_mixed, log_totals = lax.map(one_block, jnp.arange(block_total, dtype=jnp.int32))
    return (head_mixed.reshape(query_all.shape), log_totals)


def attend_backward(query_all, key_all, value_all, grad_mixed, log_totals, segments, score_scale):
    group_len = segments.shape[1]
    block_total = query_all.shape[0] // QBLOCK

    def one_block(block_index, grads):
        grad_query, grad_key, grad_value = grads
        first_row, key_start, query_rows, key_rows, value_rows, scores = block_inputs(
            block_index, segments, query_all, key_all, value_all, score_scale
        )
        weights = jnp.exp(scores - log_totals[block_index][..., None])
        grad_rows = lax.dynamic_slice_in_dim(grad_mixed, first_row, QBLOCK, 0)
        grad_weights = jnp.einsum(
            "bhe,ghe->hbg", grad_rows, value_rows, preferred_element_type=jnp.float32
        )
        grad_scores = weights * (
            grad_weights - jnp.sum(weights * grad_weights, axis=-1, keepdims=True)
        )
        grad_scores = grad_scores.astype(jnp.bfloat16)
        part_query = (
            jnp.einsum("hbg,ghe->bhe", grad_scores, key_rows, preferred_element_type=jnp.float32)
            * score_scale
        )
        part_key = (
            jnp.einsum("hbg,bhe->ghe", grad_scores, query_rows, preferred_element_type=jnp.float32)
            * score_scale
        )
        part_value = jnp.einsum(
            "hbg,bhe->ghe",
            weights.astype(jnp.bfloat16),
            grad_rows,
            preferred_element_type=jnp.float32,
        )
        grad_query = lax.dynamic_update_slice_in_dim(grad_query, part_query, first_row, 0)
        old_key = lax.dynamic_slice_in_dim(grad_key, key_start, group_len, 0)
        grad_key = lax.dynamic_update_slice_in_dim(grad_key, old_key + part_key, key_start, 0)
        old_value = lax.dynamic_slice_in_dim(grad_value, key_start, group_len, 0)
        grad_value = lax.dynamic_update_slice_in_dim(
            grad_value, old_value + part_value, key_start, 0
        )
        return (grad_query, grad_key, grad_value)

    zero_rows = jnp.zeros(query_all.shape, jnp.float32)
    return lax.fori_loop(0, block_total, one_block, (zero_rows, zero_rows, zero_rows))


def shards(
    tokens,
    segment_ids,
    memory_positions,
    memory_rows,
    qkv_weight,
    qv_bias,
    out_weight,
    out_bias,
    norm1_gain,
    norm1_bias,
    up_weight,
    up_bias,
    down_weight,
    down_bias,
    norm2_gain,
    norm2_bias,
    out_cotangent,
):
    row_count, model_width = tokens.shape
    group_count, group_len = segment_ids.shape
    head_dim = out_weight.shape[2]
    score_scale = float(head_dim) ** (-0.5)
    row_place = lax.axis_index("tensor") * row_count + jnp.arange(row_count, dtype=jnp.int32)
    targets = (
        memory_positions + group_len * jnp.arange(group_count, dtype=jnp.int32)[:, None]
    ).reshape(-1)
    memory_picks = (row_place[:, None] == targets[None, :]).astype(jnp.float32)
    memory_table = jnp.tile(memory_rows.astype(jnp.float32), (group_count, 1))
    inputs = tokens.astype(jnp.float32) + jnp.dot(
        memory_picks, memory_table, precision=lax.Precision.HIGHEST
    )
    w_qkv, w_out, w_up, w_down = (
        lax.all_gather(qkv_weight, "dp", axis=0, tiled=True),
        lax.all_gather(out_weight, "dp", axis=0, tiled=True),
        lax.all_gather(up_weight, "dp", axis=0, tiled=True),
        lax.all_gather(down_weight, "dp", axis=0, tiled=True),
    )
    gain_one = norm1_gain.astype(jnp.float32)
    shift_one = norm1_bias.astype(jnp.float32)
    gain_two = norm2_gain.astype(jnp.float32)
    shift_two = norm2_bias.astype(jnp.float32)
    inputs_low = inputs.astype(jnp.bfloat16)
    all_inputs = lax.all_gather(inputs_low, "tensor", axis=0, tiled=True)
    bias_query = qv_bias[:, :head_dim].astype(jnp.float32)
    bias_value = qv_bias[:, head_dim:].astype(jnp.float32)
    qkv_bias = jnp.concatenate([bias_query, jnp.zeros_like(bias_query), bias_value], axis=-1)
    projected = (
        jnp.einsum("td,dhe->the", all_inputs, w_qkv, preferred_element_type=jnp.float32) + qkv_bias
    )
    projected = projected.astype(jnp.bfloat16)
    query_all = projected[..., :head_dim]
    key_all = projected[..., head_dim : 2 * head_dim]
    value_all = projected[..., 2 * head_dim :]
    head_mixed, log_totals = attend_forward(query_all, key_all, value_all, segment_ids, score_scale)
    row_piece = head_mixed
    attended = lax.psum_scatter(
        jnp.einsum("the,dhe->td", row_piece, w_out, preferred_element_type=jnp.float32),
        "tensor",
        scatter_dimension=0,
        tiled=True,
    ) + out_bias.astype(jnp.float32)
    first_sum = inputs + attended
    hidden = layer_norm(first_sum, gain_one, shift_one)
    hidden_low = hidden.astype(jnp.bfloat16)
    all_hidden = lax.all_gather(hidden_low, "tensor", axis=0, tiled=True)
    pre_act = jnp.dot(all_hidden, w_up, preferred_element_type=jnp.float32) + up_bias.astype(
        jnp.float32
    )
    activated = gelu_exact(pre_act).astype(jnp.bfloat16)
    row_piece = activated
    branch = lax.psum_scatter(
        jnp.einsum("tf,df->td", row_piece, w_down, preferred_element_type=jnp.float32),
        "tensor",
        scatter_dimension=0,
        tiled=True,
    )
    second_sum = hidden + branch + down_bias.astype(jnp.float32)
    block_out = layer_norm(second_sum, gain_two, shift_two).astype(jnp.bfloat16)
    cotangent = out_cotangent.astype(jnp.float32)
    _, norm_two_back = jax.vjp(layer_norm, second_sum, gain_two, shift_two)
    grad_second, grad_gain_two, grad_shift_two = norm_two_back(cotangent)
    grad_branch_low = grad_second.astype(jnp.bfloat16)
    grad_down_bias = jnp.sum(grad_branch_low.astype(jnp.float32), axis=0)
    all_grad_branch = lax.all_gather(grad_branch_low, "tensor", axis=0, tiled=True)
    grad_act = jnp.einsum("td,df->tf", all_grad_branch, w_down, preferred_element_type=jnp.float32)
    grad_down = jnp.einsum(
        "td,tf->df", all_grad_branch, activated, preferred_element_type=jnp.float32
    )
    grad_pre = jax.vjp(gelu_exact, pre_act)[1](grad_act)[0].astype(jnp.bfloat16)
    grad_up = jnp.einsum("td,tf->df", all_hidden, grad_pre, preferred_element_type=jnp.float32)
    grad_up_bias = jnp.sum(grad_pre.astype(jnp.float32), axis=0)
    row_piece = grad_pre
    grad_hidden = (
        lax.psum_scatter(
            jnp.einsum("tf,df->td", row_piece, w_up, preferred_element_type=jnp.float32),
            "tensor",
            scatter_dimension=0,
            tiled=True,
        )
        + grad_second
    )
    _, norm_one_back = jax.vjp(layer_norm, first_sum, gain_one, shift_one)
    grad_first, grad_gain_one, grad_shift_one = norm_one_back(grad_hidden)
    grad_attended_low = grad_first.astype(jnp.bfloat16)
    grad_out_bias = jnp.sum(grad_attended_low.astype(jnp.float32), axis=0)
    all_grad_attended = lax.all_gather(grad_attended_low, "tensor", axis=0, tiled=True)
    grad_mixed = jnp.einsum(
        "td,dhe->the", all_grad_attended, w_out, preferred_element_type=jnp.float32
    ).astype(jnp.bfloat16)
    grad_out = jnp.einsum(
        "td,the->dhe", all_grad_attended, head_mixed, preferred_element_type=jnp.float32
    )
    grad_query, grad_key, grad_value = attend_backward(
        query_all, key_all, value_all, grad_mixed, log_totals, segment_ids, score_scale
    )
    grad_projected = jnp.concatenate([grad_query, grad_key, grad_value], axis=-1).astype(
        jnp.bfloat16
    )
    grad_qkv = jnp.einsum(
        "td,the->dhe", all_inputs, grad_projected, preferred_element_type=jnp.float32
    )
    bias_sums = jnp.sum(grad_projected.astype(jnp.float32), axis=0)
    grad_qv_bias = jnp.concatenate([bias_sums[:, :head_dim], bias_sums[:, 2 * head_dim :]], axis=-1)
    row_piece = grad_projected
    grad_tokens = (
        lax.psum_scatter(
            jnp.einsum("the,dhe->td", row_piece, w_qkv, preferred_element_type=jnp.float32).astype(
                jnp.bfloat16
            ),
            "tensor",
            scatter_dimension=0,
            tiled=True,
        ).astype(jnp.float32)
        + grad_first
    )
    grad_memory = jnp.dot(memory_picks.T, grad_tokens, precision=lax.Precision.HIGHEST)
    grad_memory = jnp.sum(grad_memory.reshape(group_count, -1, model_width), axis=0)
    grad_qkv, grad_out, grad_up, grad_down = (
        lax.psum_scatter(grad_qkv, "dp", scatter_dimension=0, tiled=True),
        lax.psum_scatter(grad_out, "dp", scatter_dimension=0, tiled=True),
        lax.psum_scatter(grad_up, "dp", scatter_dimension=0, tiled=True),
        lax.psum_scatter(grad_down, "dp", scatter_dimension=0, tiled=True),
    )
    grad_qv_bias, grad_up_bias = lax.psum((grad_qv_bias, grad_up_bias), "dp")
    (
        grad_memory,
        grad_out_bias,
        grad_gain_one,
        grad_shift_one,
        grad_down_bias,
        grad_gain_two,
        grad_shift_two,
    ) = lax.psum(
        (
            grad_memory,
            grad_out_bias,
            grad_gain_one,
            grad_shift_one,
            grad_down_bias,
            grad_gain_two,
            grad_shift_two,
        ),
        ("dp", "tensor"),
    )
    return (
        block_out,
        grad_tokens,
        grad_memory,
        grad_qkv,
        grad_qv_bias,
        grad_out,
        grad_out_bias,
        grad_gain_one,
        grad_shift_one,
        grad_up,
        grad_up_bias,
        grad_down,
        grad_down_bias,
        grad_gain_two,
        grad_shift_two,
    )


def solution(mesh):
    in_specs = (
        P(("dp", "tensor"), None),
        P("dp", None),
        P("dp", None),
        P(),
        P("dp", "tensor", None),
        P("tensor", None),
        P("dp", "tensor", None),
        P(),
        P(),
        P(),
        P("dp", "tensor"),
        P("tensor"),
        P("dp", "tensor"),
        P(),
        P(),
        P(),
        P(("dp", "tensor"), None),
    )
    out_specs = (
        P(("dp", "tensor"), None),
        P(("dp", "tensor"), None),
        P(),
        P("dp", "tensor", None),
        P("tensor", None),
        P("dp", "tensor", None),
        P(),
        P(),
        P(),
        P("dp", "tensor"),
        P("tensor"),
        P("dp", "tensor"),
        P(),
        P(),
        P(),
    )
    return jax.shard_map(shards, mesh=mesh, in_specs=in_specs, out_specs=out_specs, check_vma=False)
```

profile of v0, /device:TPU:0, one launch (start us, length us, event | category | flops | bytes accessed | tf_op | source)
XLA Modules:
  0.0 1528.1 jit_solution(10689661794506984223)
XLA Ops:
  15.6 39.0 %all_gather.25 = bf16[768,3,192]{2,1,0:T(4,128)(2,1)S(1)} all-gather(bf16[96,3,192]{2,1,0:T(4,128)(2,1)S(1)} %copy.60), channel_id=1, replica_groups=mesh['dp'=8,'tensor'=4] {'dp'}, dimensions={0}, use_global_device_ids=true | all-gather | bytes 995328 | tf_op jit(solution)/shard_map/all_gather | solution.py:139
  55.6 32.3 %all_gather.26 = bf16[768,3,64]{2,1,0:T(4,128)(2,1)S(1)} all-gather(bf16[96,3,64]{2,1,0:T(4,128)(2,1)S(1)} %copy.64), channel_id=1, replica_groups=mesh['dp'=8,'tensor'=4] {'dp'}, dimensions={0}, use_global_device_ids=true | all-gather | bytes 331776 | tf_op jit(solution)/shard_map/all_gather | solution.py:140
  98.0 205.0 %while.35 = (s32[]{:T(128)}, bf16[8,512,3,64]{1,3,2,0:T(8,128)(2,1)}, f32[8,3,512]{2,1,0:T(4,128)}, s32[8]{0:T(128)S(1)}, bf16[4096,3,64]{0,2,1:T(8,128)(2,1)}, ...) while((s32[]{:T(128)}, ...), condition=%wide.region_3.4_spmd, body=%wide.region_0.3_spmd.sunk | while | flops 845251072 | bytes 50292328 | solution.py:57
  116.3 7.3 fusion.129
  141.9 7.3 fusion.129
  167.6 7.3 fusion.129
  193.2 7.3 fusion.129
  218.8 7.3 fusion.129
  244.4 7.3 fusion.129
  270.1 7.3 fusion.129
  295.7 7.3 fusion.129
  312.8 95.4 %reduce-scatter.11.cloned.1.call-done = f32[1024,768]{0,1:T(8,128)} async-done(((f32[4096,768]{0,1:T(8,128)}), f32[1024,768]{0,1:T(8,128)}) %reduce-scatter.11.cloned.1.call-update) | async-done | bytes 3145744 | tf_op jit(solution)/shard_map/reduce_scatter | solution.py:162
  414.9 45.6 %all-gather.9.cloned.1.call-done = bf16[4096,768]{0,1:T(8,128)(2,1)} async-done(((bf16[1024,768]{0,1:T(8,128)(2,1)}), bf16[4096,768]{0,1:T(8,128)(2,1)}) %all-gather.9.cloned.1.call-update) | async-done | bytes 6291472 | tf_op jit(solution)/shard_map/all_gather | solution.py:171
  460.5 35.6 %multiply_convert_fusion.1 = (bf16[4096,768]{1,0:T(8,128)(2,1)}, f32[4096,768]{1,0:T(8,128)}, f32[4096,768]{1,0:T(8,128)}) fusion(f32[768]{0:T(1024)S(1)} %convert_element_type.132, bf16[4096,768]{0,1:T(8,128)(2,1)} %all-gather.9.cloned.1.call-done, bf16[768,768]{1,0:T(8,128)(2,1)} %all-gather.11.cloned.1.call-done), kind=kOutput, calls=%fused_computation.62 | convolution fusion | flops 5039456256 | bytes 38931456 | tf_op jit(solution)/shard_map/dot_general | solution.py:172
  496.1 7.9 all-gather.13.cloned.1.call-done
  504.0 10.1 fusion.78
  517.4 92.3 %reduce-scatter.13.cloned.1.call-done = f32[1024,768]{0,1:T(8,128)} async-done(((f32[4096,768]{0,1:T(8,128)}), f32[1024,768]{0,1:T(8,128)}) %reduce-scatter.13.cloned.1.call-update) | async-done | bytes 3145744 | tf_op jit(solution)/shard_map/reduce_scatter | solution.py:177
  619.6 46.3 %all-gather.15.cloned.1.call-done = bf16[4096,768]{0,1:T(8,128)(2,1)} async-done(((bf16[1024,768]{0,1:T(8,128)(2,1)}), bf16[4096,768]{0,1:T(8,128)(2,1)}) %all-gather.15.cloned.1.call-update) | async-done | bytes 6291472 | tf_op jit(solution)/shard_map/all_gather | solution.py:190
  665.9 19.8 %convert_reduce_fusion = (f32[768]{0:T(1024)}, bf16[4096,768]{1,0:T(8,128)(2,1)}) fusion(f32[4096,768]{1,0:T(8,128)} %get-tuple-element.552, f32[4096,768]{1,0:T(8,128)} %get-tuple-element.571, f32[768]{0:T(1024)S(1)} %convert_element_type.132, bf16[4096,768]{0,1:T(8,128)(2,1)} %all-gather.15.cloned.1.call-done, ...), kind=kOutput, calls=%fused_computation.60 | convolution fusion | flops 4885314560 | bytes 38934528 | tf_op jit(solution)/shard_map/td,df->tf/dot_general | solution.py:191
  685.7 10.7 fusion.79
  697.0 96.5 %reduce-scatter.15.cloned.1.call-done = f32[1024,768]{0,1:T(8,128)} async-done(((f32[4096,768]{0,1:T(8,128)}), f32[1024,768]{0,1:T(8,128)}) %reduce-scatter.15.cloned.1.call-update) | async-done | bytes 3145744 | tf_op jit(solution)/shard_map/reduce_scatter | solution.py:200
  805.9 45.1 %all-gather.17.cloned.1.call-done = bf16[4096,768]{0,1:T(8,128)(2,1)} async-done(((bf16[1024,768]{0,1:T(8,128)(2,1)}), bf16[4096,768]{0,1:T(8,128)(2,1)}) %all-gather.17.cloned.1.call-update) | async-done | bytes 6291472 | tf_op jit(solution)/shard_map/all_gather | solution.py:212
  860.7 294.6 %while.36 = (s32[]{:T(128)}, bf16[4096,3,64]{0,2,1:T(8,128)(2,1)}, f32[4096,3,64]{0,2,1:T(8,128)}, f32[4096,3,64]{0,2,1:T(8,128)}, bf16[4096,3,64]{0,2,1:T(8,128...) while((s32[]{:T(128)}, bf16[4096,3,64]{0,2,1:T(8,128)(2,1)}, ...), condition=%wide.region_17.18_spmd, body=%wide.region_15.17_spmd.sunk | while | flops 2063827456 | bytes 181875408 | solution.py:103
  860.9 7.3 fusion.138
  870.7 7.9 multiply_reduce_fusion.6
  897.6 7.3 fusion.138
  907.5 7.9 multiply_reduce_fusion.6
  934.4 7.3 fusion.138
  944.2 7.9 multiply_reduce_fusion.6
  971.2 7.3 fusion.138
  981.0 7.9 multiply_reduce_fusion.6
  1007.9 7.3 fusion.138
  1017.7 7.9 multiply_reduce_fusion.6
  1044.7 7.3 fusion.138
  1054.5 7.9 multiply_reduce_fusion.6
  1081.4 7.3 fusion.138
  1091.3 7.9 multiply_reduce_fusion.6
  1118.2 7.3 fusion.138
  1128.0 7.9 multiply_reduce_fusion.6
  1177.3 11.4 fusion.82
  1188.8 10.6 fusion.81
  1199.6 9.8 fusion.54
  1215.0 11.4 reduce-scatter.17.cloned.1.call-done
  1232.7 22.2 %all-reduce.1 = (f32[3,128]{1,0:T(4,128)}, f32[768]{0:T(1024)}) all-reduce(f32[3,128]{1,0:T(4,128)S(1)} %pad_maximum_fusion.2, f32[768]{0:T(1024)S(1)} %copy-done.31), channel_id=1, replica_groups=mesh['dp'=8,'tensor'=4] {'dp'}, use_global_device_ids=true, to_apply=%region_23.24 | all-reduce | flops 1152 | bytes 9216 | tf_op jit(solution)/shard_map/psum | solution.py:250
  1254.9 37.9 %reduce-scatter.25.cloned.1.call-done = f32[96,192]{1,0:T(8,128)} async-done(((f32[768,192]{1,0:T(8,128)}), f32[96,192]{1,0:T(8,128)}) %reduce-scatter.25.cloned.1.call-update) | async-done | bytes 73744
  1298.0 67.8 %reduce-scatter.23.cloned.1.call-done = f32[96,768]{1,0:T(8,128)} async-done(((f32[768,768]{1,0:T(8,128)}), f32[96,768]{1,0:T(8,128)}) %reduce-scatter.23.cloned.1.call-update) | async-done | bytes 294928 | tf_op jit(solution)/shard_map/reduce_scatter | solution.py:248
  1365.8 72.8 %reduce-scatter.21.cloned.1.call-done = f32[96,768]{1,0:T(8,128)} async-done(((f32[768,768]{1,0:T(8,128)}), f32[96,768]{1,0:T(8,128)}) %reduce-scatter.21.cloned.1.call-update) | async-done | bytes 294928 | tf_op jit(solution)/shard_map/reduce_scatter | solution.py:247
  1438.6 73.0 %reduce-scatter.19.cloned.1.call-done = f32[96,3,192]{2,0,1:T(8,128)} async-done(((f32[768,3,192]{2,0,1:T(8,128)}), f32[96,3,192]{2,0,1:T(8,128)}) %reduce-scatter.19.cloned.1.call-update) | async-done | bytes 221200 | tf_op jit(solution)/shard_map/reduce_scatter | solution.py:245
  (440 shorter events, 415.6 us)
Async XLA Ops:
  8.0 80.6 %all-gather.7.cloned.1.call-start = ((), (), s32[]{:S(2)}) async-start(), calls=%async_computation.8 | async-start | bytes 7864320 | tf_op jit(solution)/shard_map/all_gather | solution.py:149
  15.4 40.1 %copy-start.23 = (bf16[96,3,64]{0,2,1:T(8,128)(2,1)S(1)}, bf16[96,3,64]{0,2,1:T(8,128)(2,1)}, u32[]{:S(2)}) copy-start(bf16[96,3,64]{0,2,1:T(8,128)(2,1)} %param.27) | copy-start | bytes 110596
  15.4 73.2 %copy-start.30 = (bf16[3,128]{1,0:T(4,128)(2,1)S(1)}, bf16[3,128]{1,0:T(4,128)(2,1)}, u32[]{:S(2)}) copy-start(bf16[3,128]{1,0:T(4,128)(2,1)} %param.26) | copy-start | bytes 2308
  15.4 392.8 %reduce-scatter.11.cloned.1.call-start = ((), (), s32[]{:S(2)}) async-start(), calls=%async_computation.9 | async-start | bytes 15728640 | tf_op jit(solution)/shard_map/reduce_scatter | solution.py:162
  55.5 39.1 %copy-start.18 = (bf16[768,3,192]{0,2,1:T(8,128)(2,1)}, bf16[768,3,192]{0,2,1:T(8,128)(2,1)S(1)}, u32[]{:S(2)}) copy-start(bf16[768,3,192]{0,2,1:T(8,128)(2,1)S(1)} %copy.62) | copy-start | bytes 2654212
  88.4 216.7 %copy-start.16 = (bf16[768,3,64]{0,2,1:T(8,128)(2,1)}, bf16[768,3,64]{0,2,1:T(8,128)(2,1)S(1)}, u32[]{:S(2)}) copy-start(bf16[768,3,64]{0,2,1:T(8,128)(2,1)S(1)} %copy.65) | copy-start | bytes 884740
  303.0 8.5 copy-start.4
  311.6 103.3 %all-gather.11.cloned.1.call-start = ((), (), s32[]{:S(2)}) async-start(), calls=%async_computation.11 | async-start | bytes 1327104 | tf_op jit(solution)/shard_map/all_gather | solution.py:141
  312.2 148.3 %all-gather.9.cloned.1.call-start = ((), (), s32[]{:S(2)}) async-start(), calls=%async_computation.10 | async-start | bytes 7864320 | tf_op jit(solution)/shard_map/all_gather | solution.py:171
  412.5 83.6 %copy-start.26 = (f32[1024]{0:T(1024)}, f32[1024]{0:T(1024)S(1)}, u32[]{:S(2)}) copy-start(f32[1024]{0:T(1024)S(1)} %multiply_reduce_fusion.4) | copy-start | bytes 12292
  414.2 89.8 %all-gather.13.cloned.1.call-start = ((), (), s32[]{:S(2)}) async-start(), calls=%async_computation.12 | async-start | bytes 1327104 | tf_op jit(solution)/shard_map/all_gather | solution.py:142
  414.7 195.0 %reduce-scatter.13.cloned.1.call-start = ((), (), s32[]{:S(2)}) async-start(), calls=%async_computation.13 | async-start | bytes 15728640 | tf_op jit(solution)/shard_map/reduce_scatter | solution.py:177
  514.2 151.7 %all-gather.15.cloned.1.call-start = ((), (), s32[]{:S(2)}) async-start(), calls=%async_computation.14 | async-start | bytes 7864320 | tf_op jit(solution)/shard_map/all_gather | solution.py:190
  619.4 174.2 %reduce-scatter.15.cloned.1.call-start = ((), (), s32[]{:S(2)}) async-start(), calls=%async_computation.15 | async-start | bytes 15728640 | tf_op jit(solution)/shard_map/reduce_scatter | solution.py:200
  665.9 19.8 %copy-start.41 = (bf16[768,768]{1,0:T(8,128)(2,1)S(1)}, bf16[768,768]{1,0:T(8,128)(2,1)}, u32[]{:S(2)}) copy-start(bf16[768,768]{1,0:T(8,128)(2,1)} %all-gather.11.cloned.1.call-done) | copy-start | bytes 3538948
  696.4 154.7 %all-gather.17.cloned.1.call-start = ((), (), s32[]{:S(2)}) async-start(), calls=%async_computation.16 | async-start | bytes 7864320 | tf_op jit(solution)/shard_map/all_gather | solution.py:212
  697.0 102.9 %copy-start.27 = (f32[1024]{0:T(1024)S(1)}, f32[1024]{0:T(1024)}, u32[]{:S(2)}) copy-start(f32[1024]{0:T(1024)} %copy-done.26) | copy-start | bytes 12292
  800.9 50.2 %copy-start.17 = (bf16[768,3,64]{0,2,1:T(8,128)(2,1)S(1)}, bf16[768,3,64]{0,2,1:T(8,128)(2,1)}, u32[]{:S(2)}) copy-start(bf16[768,3,64]{0,2,1:T(8,128)(2,1)} %copy-done.16) | copy-start | bytes 884740
  804.5 421.9 %reduce-scatter.17.cloned.1.call-start = ((), (), s32[]{:S(2)}) async-start(), calls=%async_computation.17 | async-start | bytes 7864320 | tf_op jit(solution)/shard_map/reduce_scatter | solution.py:232
  870.7 7.9 slice-start.1
  870.7 8.9 slice-start.2
  907.5 7.9 slice-start
  907.5 7.9 slice-start.1
  907.5 8.9 slice-start.2
  944.2 8.9 slice-start.2
  981.0 7.9 slice-start.1
  981.0 8.9 slice-start.2
  1017.7 7.9 slice-start.1
  1017.7 8.9 slice-start.2
  1054.5 7.9 slice-start.1
  1054.5 8.9 slice-start.2
  1091.3 7.9 slice-start
  1091.3 8.0 slice-start.1
  1091.3 8.9 slice-start.2
  1128.0 7.9 slice-start
  1128.0 8.0 slice-start.1
  1128.0 8.9 slice-start.2
  1157.6 42.0 %copy-start.14 = (bf16[4096,3,64]{0,2,1:T(8,128)(2,1)}, bf16[4096,3,64]{0,2,1:T(8,128)(2,1)S(1)}, u32[]{:S(2)}) copy-start(bf16[4096,3,64]{0,2,1:T(8,128)(2,1)S(1)} %convert.10) | copy-start | bytes 4718596
  1168.4 124.4 %reduce-scatter.25.cloned.1.call-start = ((), (), s32[]{:S(2)}) async-start(), calls=%async_computation.21 | async-start | bytes 884736
  1177.3 188.5 %reduce-scatter.23.cloned.1.call-start = ((), (), s32[]{:S(2)}) async-start(), calls=%async_computation.20 | async-start | bytes 2654208 | tf_op jit(solution)/shard_map/reduce_scatter | solution.py:248
  1188.7 249.9 %reduce-scatter.21.cloned.1.call-start = ((), (), s32[]{:S(2)}) async-start(), calls=%async_computation.19 | async-start | bytes 2654208 | tf_op jit(solution)/shard_map/reduce_scatter | solution.py:247
  1199.4 312.3 %reduce-scatter.19.cloned.1.call-start = ((), (), s32[]{:S(2)}) async-start(), calls=%async_computation.18 | async-start | bytes 2654208 | tf_op jit(solution)/shard_map/reduce_scatter | solution.py:245
  1209.4 17.0 %copy-start.9 = (f32[1024,768]{0,1:T(8,128)S(1)}, f32[1024,768]{0,1:T(8,128)}, u32[]{:S(2)}) copy-start(f32[1024,768]{0,1:T(8,128)} %copy-done.8) | copy-start | bytes 9437188
  1209.4 17.0 %copy-start.25 = (f32[1024]{0:T(1024)S(1)}, f32[1024]{0:T(1024)}, u32[]{:S(2)}) copy-start(f32[1024]{0:T(1024)} %copy-done.24) | copy-start | bytes 12292
  1209.4 302.2 %all-reduce.4.cloned.1.call-start = ((), (), s32[]{:S(2)}) async-start(), calls=%async_computation.22 | async-start | bytes 196608 | tf_op jit(solution)/shard_map/psum | solution.py:259
  1215.0 15.1 copy-start.29
  1215.0 15.1 copy-start.40
  1215.0 17.7 %copy-start.31 = (f32[768]{0:T(1024)S(1)}, f32[768]{0:T(1024)}, u32[]{:S(2)}) copy-start(f32[768]{0:T(1024)} %get-tuple-element.540) | copy-start | bytes 9220
  (68 other events, 284.4 us)
Sparse Core Ops, SparseCore 0:
  15.5 49.0 all-gather.6
  311.7 96.4 reduce-scatter.10
  619.5 46.3 all-gather.14
  804.7 46.3 all-gather.16
  1168.5 57.8 reduce-scatter.16
  1229.6 63.2 reduce-scatter.24
  1296.9 68.8 reduce-scatter.22
  1369.9 68.6 reduce-scatter.20
  1442.7 68.8 reduce-scatter.18
Sparse Core Ops, SparseCore 1:
  314.3 40.7 all-gather.10
  414.3 46.2 all-gather.8
  462.6 41.4 all-gather.12
  514.3 95.4 reduce-scatter.12
  696.4 97.0 reduce-scatter.14
  1232.7 132.7 all-reduce.3
where the time goes:
time: 1530 us
  waiting for transfers between devices  693 us (45%)
  matrix products  468 us (31%)
  other arithmetic  160 us (10%)
  blocking collectives  93.5 us (6%)
  local copies, waits for them, and re-layouts  73 us (5%)
  loops' own time  22.4 us (1%)
  between operations  16.2 us (1%)
    dot_general x16, matrix products, block_inputs(): jnp.einsum('bhe,ghe->hbg', query_rows, key_rows, preferred_element_type=j...  112 us
    reduce_scatter x1, waiting for transfers between devices, shards(): lax.psum_scatter(jnp.einsum('tf,df->td', row_piece, w_up, preferred_eleme...  96.5 us
    reduce_scatter x1, waiting for transfers between devices, shards(): lax.psum_scatter(jnp.einsum('the,dhe->td', row_piece, w_out, preferred_el...  95.4 us
    reduce_scatter x1, waiting for transfers between devices, shards(): lax.psum_scatter(jnp.einsum('tf,df->td', row_piece, w_down, preferred_ele...  92.3 us
    reduce_scatter x1, waiting for transfers between devices, shards(): lax.psum_scatter(grad_qkv, 'dp', scatter_dimension=0, tiled=True)  73 us
    reduce_scatter x1, waiting for transfers between devices, shards(): lax.psum_scatter(grad_up, 'dp', scatter_dimension=0, tiled=True)  72.8 us
    reduce_scatter x1, waiting for transfers between devices, shards(): lax.psum_scatter(grad_down, 'dp', scatter_dimension=0, tiled=True)  67.8 us
    dot_general x8, matrix products, one_block(): jnp.einsum('bhe,ghe->hbg', grad_rows, value_rows, preferred_element_type=...  63.4 us
  transfers between devices with their start and end apart: 15, of which 12 were waited for; matrix products, arithmetic and copies ran while one was open for 7% of the time, Pallas kernels for 0%

commit v1 on v0

--- a/solution.py
+++ b/solution.py
@@ -6,6 +6,25 @@
 QBLOCK = 512
 EPSILON = 1e-12
 MASKED = -1e30
+
+
+def laid_out(pieces, dim):
+    dims = list(pieces.shape[1:])
+    dims[dim] *= pieces.shape[0]
+    return jnp.moveaxis(pieces, 0, dim).reshape(dims)
+
+
+def grow_blocks(x, axis):
+    size, index = (lax.axis_size(axis), lax.axis_index(axis))
+    blocks, stride = (x[None], 1)
+    while stride < size:
+        received = lax.ppermute(blocks, axis, [(i, i ^ stride) for i in range(size)])
+        low = index & stride == 0
+        blocks = jnp.concatenate(
+            [jnp.where(low, blocks, received), jnp.where(low, received, blocks)]
+        )
+        stride *= 2
+    return blocks
 
 
 def layer_norm(values, norm_gain, norm_shift):
@@ -187,7 +206,7 @@
     grad_second, grad_gain_two, grad_shift_two = norm_two_back(cotangent)
     grad_branch_low = grad_second.astype(jnp.bfloat16)
     grad_down_bias = jnp.sum(grad_branch_low.astype(jnp.float32), axis=0)
-    all_grad_branch = lax.all_gather(grad_branch_low, "tensor", axis=0, tiled=True)
+    all_grad_branch = laid_out(grow_blocks(grad_branch_low, "tensor"), 0)
     grad_act = jnp.einsum("td,df->tf", all_grad_branch, w_down, preferred_element_type=jnp.float32)
     grad_down = jnp.einsum(
         "td,tf->df", all_grad_branch, activated, preferred_element_type=jnp.float32

time: 1530 us -> 1580 us (1.033)
  waiting for transfers between devices: 693 us -> 740 us
    ppermute x0 -> x2, waiting for transfers between devices: none -> 73.8 us  [grow_blocks(): lax.ppermute(blocks, axis, [(i, i ^ stride) for i in range(size)])]
    all_gather x1 -> x0, waiting for transfers between devices: 46.3 us -> none  [shards(): lax.all_gather(grad_branch_low, 'tensor', axis=0, tiled=True)]
    unnamed x16 -> x15, waiting for transfers between devices: 39.2 us -> 39.9 us
  transfers between devices with their start and end apart: 15 -> 16, of which waited for: 12 -> 13; matrix products, arithmetic and copies ran while one was open for 7% -> 6% of each run, Pallas kernels for 0% -> 0%
where the time goes in v1:
time: 1580 us
  waiting for transfers between devices  740 us (47%)
  matrix products  469 us (30%)
  other arithmetic  169 us (11%)
  blocking collectives  93.7 us (6%)
  local copies, waits for them, and re-layouts  65.4 us (4%)
  loops' own time  22.2 us (1%)
  between operations  16.2 us (1%)
    dot_general x16, matrix products, block_inputs(): jnp.einsum('bhe,ghe->hbg', query_rows, key_rows, preferred_element_type=j...  113 us
    reduce_scatter x1, waiting for transfers between devices, shards(): lax.psum_scatter(jnp.einsum('tf,df->td', row_piece, w_up, preferred_eleme...  99.7 us
    reduce_scatter x1, waiting for transfers between devices, shards(): lax.psum_scatter(jnp.einsum('the,dhe->td', row_piece, w_out, preferred_el...  98 us
    reduce_scatter x1, waiting for transfers between devices, shards(): lax.psum_scatter(jnp.einsum('tf,df->td', row_piece, w_down, preferred_ele...  97.5 us
    ppermute x2, waiting for transfers between devices, grow_blocks(): lax.ppermute(blocks, axis, [(i, i ^ stride) for i in range(size)])  73.8 us
    reduce_scatter x1, waiting for transfers between devices, shards(): lax.psum_scatter(grad_qkv, 'dp', scatter_dimension=0, tiled=True)  73 us
    reduce_scatter x1, waiting for transfers between devices, shards(): lax.psum_scatter(grad_up, 'dp', scatter_dimension=0, tiled=True)  73 us
    reduce_scatter x1, waiting for transfers between devices, shards(): lax.psum_scatter(grad_down, 'dp', scatter_dimension=0, tiled=True)  71.4 us
  transfers between devices with their start and end apart: 16, of which 13 were waited for; matrix products, arithmetic and copies ran while one was open for 6% of the time, Pallas kernels for 0%

profile of v1, /device:TPU:0, one launch (start us, length us, event | category | flops | bytes accessed | tf_op | source)
XLA Modules:
  0.0 1577.1 jit_solution(7030995944538535196)
XLA Ops:
  15.1 39.2 %all_gather.22 = bf16[768,3,192]{2,1,0:T(4,128)(2,1)S(1)} all-gather(bf16[96,3,192]{2,1,0:T(4,128)(2,1)S(1)} %copy.39), channel_id=1, replica_groups=mesh['dp'=8,'tensor'=4] {'dp'}, dimensions={0}, use_global_device_ids=true | all-gather | bytes 995328 | tf_op jit(solution)/shard_map/all_gather | solution.py:158
  55.3 32.1 %all_gather.23 = bf16[768,3,64]{2,1,0:T(4,128)(2,1)S(1)} all-gather(bf16[96,3,64]{2,1,0:T(4,128)(2,1)S(1)} %copy.42), channel_id=1, replica_groups=mesh['dp'=8,'tensor'=4] {'dp'}, dimensions={0}, use_global_device_ids=true | all-gather | bytes 331776 | tf_op jit(solution)/shard_map/all_gather | solution.py:159
  98.2 205.7 %while.35 = (s32[]{:T(128)}, bf16[8,512,3,64]{1,3,2,0:T(8,128)(2,1)}, f32[8,3,512]{2,1,0:T(4,128)}, s32[8]{0:T(128)S(1)}, bf16[4096,3,64]{0,2,1:T(8,128)(2,1)}, ...) while((s32[]{:T(128)}, ...), condition=%wide.region_3.4_spmd, body=%wide.region_0.3_spmd.sunk | while | flops 845251072 | bytes 50292328 | solution.py:76
  116.6 7.3 fusion.130
  142.3 7.3 fusion.130
  168.0 7.3 fusion.130
  193.7 7.3 fusion.130
  219.4 7.3 fusion.130
  245.1 7.3 fusion.130
  270.9 7.3 fusion.130
  296.6 7.3 fusion.130
  313.4 98.0 %reduce-scatter.11.cloned.1.call-done = f32[1024,768]{1,0:T(8,128)} async-done(((f32[4096,768]{1,0:T(8,128)}), f32[1024,768]{1,0:T(8,128)}) %reduce-scatter.11.cloned.1.call-update) | async-done | bytes 3145744 | tf_op jit(solution)/shard_map/reduce_scatter | solution.py:181
  418.7 45.7 %all-gather.8.cloned.1.call-done = bf16[4096,768]{1,0:T(8,128)(2,1)} async-done(((bf16[1024,768]{1,0:T(8,128)(2,1)}), bf16[4096,768]{1,0:T(8,128)(2,1)}) %all-gather.8.cloned.1.call-update) | async-done | bytes 6291472 | tf_op jit(solution)/shard_map/all_gather | solution.py:190
  464.4 34.8 %multiply_convert_fusion.1 = (bf16[4096,768]{1,0:T(8,128)(2,1)}, f32[4096,768]{1,0:T(8,128)}, f32[4096,768]{1,0:T(8,128)}) fusion(f32[768]{0:T(1024)S(1)} %convert_element_type.132, bf16[4096,768]{1,0:T(8,128)(2,1)} %all-gather.8.cloned.1.call-done, bf16[768,768]{1,0:T(8,128)(2,1)} %all-gather.10.cloned.1.call-done), kind=kOutput, calls=%fused_computation.62 | convolution fusion | flops 5039456256 | bytes 38931456 | tf_op jit(solution)/shard_map/dot_general | solution.py:191
  499.2 8.7 all-gather.12.cloned.1.call-done
  507.9 10.3 fusion.80
  518.8 97.5 %reduce-scatter.13.cloned.1.call-done = f32[1024,768]{1,0:T(8,128)} async-done(((f32[4096,768]{1,0:T(8,128)}), f32[1024,768]{1,0:T(8,128)}) %reduce-scatter.13.cloned.1.call-update) | async-done | bytes 3145744 | tf_op jit(solution)/shard_map/reduce_scatter | solution.py:196
  637.4 70.1 %collective-permute-done.1 = bf16[2,1024,768]{2,1,0:T(8,128)(2,1)} collective-permute-done((bf16[2,1024,768]{2,1,0:T(8,128)(2,1)}, bf16[2,1024,768]{2,1,0:T(8,128)(2,1)}, u32[]{:S(2)}, u32[]{:S(2)}) %collective-permute-start.1) | collective-permute-done | bytes 3145760 | tf_op jit(solution)/shard_map/ppermute | solution.py:21
  713.8 18.2 %convert_reduce_fusion = (f32[768]{0:T(1024)}, bf16[4096,768]{1,0:T(8,128)(2,1)}) fusion(f32[4096,768]{1,0:T(8,128)} %get-tuple-element.507, f32[4096,768]{1,0:T(8,128)} %get-tuple-element.528, f32[768]{0:T(1024)S(1)} %convert_element_type.132, bf16[4096,768]{1,0:T(8,128)(2,1)} %bitcast.114, bf16[768,768]{1,0:T(8,128)(2,1)S(1)} %copy-done.43), kind=kOutput, calls=%fused_computation.60 | convolution fusion | flops 4885314560 | bytes 38934528 | tf_op jit(solution)/shard_map/td,df->tf/dot_general | solution.py:210
  731.9 10.6 fusion.81
  742.6 99.7 %reduce-scatter.15.cloned.1.call-done = f32[1024,768]{1,0:T(8,128)} async-done(((f32[4096,768]{1,0:T(8,128)}), f32[1024,768]{1,0:T(8,128)}) %reduce-scatter.15.cloned.1.call-update) | async-done | bytes 3145744 | tf_op jit(solution)/shard_map/reduce_scatter | solution.py:219
  853.2 44.9 %all-gather.14.cloned.1.call-done = bf16[4096,768]{1,0:T(8,128)(2,1)} async-done(((bf16[1024,768]{1,0:T(8,128)(2,1)}), bf16[4096,768]{1,0:T(8,128)(2,1)}) %all-gather.14.cloned.1.call-update) | async-done | bytes 6291472 | tf_op jit(solution)/shard_map/all_gather | solution.py:231
  908.6 294.3 %while.36 = (s32[]{:T(128)}, bf16[4096,3,64]{0,2,1:T(8,128)(2,1)}, f32[4096,3,64]{0,2,1:T(8,128)}, f32[4096,3,64]{0,2,1:T(8,128)}, bf16[4096,3,64]{0,2,1:T(8,128...) while((s32[]{:T(128)}, bf16[4096,3,64]{0,2,1:T(8,128)(2,1)}, ...), condition=%wide.region_17.18_spmd, body=%wide.region_15.17_spmd.sunk | while | flops 2063827456 | bytes 181875408 | solution.py:122
  908.7 7.3 fusion.139
  918.6 7.9 multiply_reduce_fusion.6
  945.5 7.3 fusion.139
  955.3 7.9 multiply_reduce_fusion.6
  982.3 7.3 fusion.139
  992.1 7.9 multiply_reduce_fusion.6
  1019.0 7.3 fusion.139
  1028.8 7.9 multiply_reduce_fusion.6
  1055.7 7.3 fusion.139
  1065.5 7.9 multiply_reduce_fusion.6
  1092.4 7.3 fusion.139
  1102.3 7.9 multiply_reduce_fusion.6
  1129.2 7.3 fusion.139
  1139.0 7.9 multiply_reduce_fusion.6
  1165.9 7.3 fusion.139
  1175.7 7.9 multiply_reduce_fusion.6
  1225.7 11.1 fusion.84
  1236.8 10.9 fusion.83
  1248.1 9.8 fusion.54
  1260.9 13.9 reduce-scatter.17.cloned.1.call-done
  1280.5 22.3 %all-reduce.1 = (f32[3,128]{1,0:T(4,128)}, f32[768]{0:T(1024)}) all-reduce(f32[3,128]{1,0:T(4,128)S(1)} %pad_maximum_fusion.4, f32[768]{0:T(1024)S(1)} %copy-done.32), channel_id=1, replica_groups=mesh['dp'=8,'tensor'=4] {'dp'}, use_global_device_ids=true, to_apply=%region_23.24 | all-reduce | flops 1152 | bytes 9216 | tf_op jit(solution)/shard_map/psum | solution.py:269
  1302.8 38.7 %reduce-scatter.25.cloned.1.call-done = f32[96,192]{1,0:T(8,128)} async-done(((f32[768,192]{1,0:T(8,128)}), f32[96,192]{1,0:T(8,128)}) %reduce-scatter.25.cloned.1.call-update) | async-done | bytes 73744
  1343.1 71.4 %reduce-scatter.23.cloned.1.call-done = f32[96,768]{1,0:T(8,128)} async-done(((f32[768,768]{1,0:T(8,128)}), f32[96,768]{1,0:T(8,128)}) %reduce-scatter.23.cloned.1.call-update) | async-done | bytes 294928 | tf_op jit(solution)/shard_map/reduce_scatter | solution.py:267
  1414.5 73.0 %reduce-scatter.21.cloned.1.call-done = f32[96,768]{1,0:T(8,128)} async-done(((f32[768,768]{1,0:T(8,128)}), f32[96,768]{1,0:T(8,128)}) %reduce-scatter.21.cloned.1.call-update) | async-done | bytes 294928 | tf_op jit(solution)/shard_map/reduce_scatter | solution.py:266
  1487.6 73.0 %reduce-scatter.19.cloned.1.call-done = f32[96,3,192]{2,0,1:T(8,128)} async-done(((f32[768,3,192]{2,0,1:T(8,128)}), f32[96,3,192]{2,0,1:T(8,128)}) %reduce-scatter.19.cloned.1.call-update) | async-done | bytes 221200 | tf_op jit(solution)/shard_map/reduce_scatter | solution.py:264
  (447 shorter events, 424.6 us)
Async XLA Ops:
  8.0 80.7 %all-gather.6.cloned.1.call-start = ((), (), s32[]{:S(2)}) async-start(), calls=%async_computation.8 | async-start | bytes 7864320 | tf_op jit(solution)/shard_map/all_gather | solution.py:168
  14.8 40.4 %copy-start.24 = (bf16[96,3,64]{0,2,1:T(8,128)(2,1)S(1)}, bf16[96,3,64]{0,2,1:T(8,128)(2,1)}, u32[]{:S(2)}) copy-start(bf16[96,3,64]{0,2,1:T(8,128)(2,1)} %param.27) | copy-start | bytes 110596
  14.8 73.8 %copy-start.31 = (bf16[3,128]{1,0:T(4,128)(2,1)S(1)}, bf16[3,128]{1,0:T(4,128)(2,1)}, u32[]{:S(2)}) copy-start(bf16[3,128]{1,0:T(4,128)(2,1)} %param.26) | copy-start | bytes 2308
  14.9 396.5 %reduce-scatter.11.cloned.1.call-start = ((), (), s32[]{:S(2)}) async-start(), calls=%async_computation.9 | async-start | bytes 15728640 | tf_op jit(solution)/shard_map/reduce_scatter | solution.py:181
  55.2 39.5 %copy-start.19 = (bf16[768,3,192]{0,2,1:T(8,128)(2,1)}, bf16[768,3,192]{0,2,1:T(8,128)(2,1)S(1)}, u32[]{:S(2)}) copy-start(bf16[768,3,192]{0,2,1:T(8,128)(2,1)S(1)} %copy.40) | copy-start | bytes 2654212
  98.2 207.8 %copy-start.17 = (bf16[768,3,64]{0,2,1:T(8,128)(2,1)S(1)}, bf16[768,3,64]{0,2,1:T(8,128)(2,1)}, u32[]{:S(2)}) copy-start(bf16[768,3,64]{0,2,1:T(8,128)(2,1)} %copy.43) | copy-start | bytes 884740
  303.9 8.6 copy-start.3
  312.5 106.2 %all-gather.10.cloned.1.call-start = ((), (), s32[]{:S(2)}) async-start(), calls=%async_computation.11 | async-start | bytes 1327104 | tf_op jit(solution)/shard_map/all_gather | solution.py:160
  313.1 151.3 %all-gather.8.cloned.1.call-start = ((), (), s32[]{:S(2)}) async-start(), calls=%async_computation.10 | async-start | bytes 7864320 | tf_op jit(solution)/shard_map/all_gather | solution.py:190
  418.0 89.8 %all-gather.12.cloned.1.call-start = ((), (), s32[]{:S(2)}) async-start(), calls=%async_computation.12 | async-start | bytes 1327104 | tf_op jit(solution)/shard_map/all_gather | solution.py:161
  418.6 197.7 %reduce-scatter.13.cloned.1.call-start = ((), (), s32[]{:S(2)}) async-start(), calls=%async_computation.13 | async-start | bytes 15728640 | tf_op jit(solution)/shard_map/reduce_scatter | solution.py:196
  518.2 324.2 %reduce-scatter.15.cloned.1.call-start = ((), (), s32[]{:S(2)}) async-start(), calls=%async_computation.14 | async-start | bytes 15728640 | tf_op jit(solution)/shard_map/reduce_scatter | solution.py:219
  628.1 3.8 collective-permute-start
  637.0 70.5 %collective-permute-start.1 = (bf16[2,1024,768]{2,1,0:T(8,128)(2,1)}, bf16[2,1024,768]{2,1,0:T(8,128)(2,1)}, u32[]{:S(2)}, u32[]{:S(2)}) collective-permute-start(bf16[2,1024,768]{2,1,0:T(8,128)(2,1)} %pad_maximum_fusion.2), channel_id=1, source_target_pairs={{0,2},{1,3},{2,0},{3,1},{4,6},{5,7},{6,4},{7,5},{8,10},{9,11},{10,... | collective-permute-start | bytes 9437192 | tf_op jit(solution)/shard_map/ppermute | solution.py:21
  713.8 18.2 %copy-start.42 = (bf16[768,768]{1,0:T(8,128)(2,1)S(1)}, bf16[768,768]{1,0:T(8,128)(2,1)}, u32[]{:S(2)}) copy-start(bf16[768,768]{1,0:T(8,128)(2,1)} %all-gather.10.cloned.1.call-done) | copy-start | bytes 3538948
  742.5 104.1 %copy-start.28 = (f32[1024]{0:T(1024)S(1)}, f32[1024]{0:T(1024)}, u32[]{:S(2)}) copy-start(f32[1024]{0:T(1024)} %copy-done.27) | copy-start | bytes 12292
  742.6 155.6 %all-gather.14.cloned.1.call-start = ((), (), s32[]{:S(2)}) async-start(), calls=%async_computation.15 | async-start | bytes 7864320 | tf_op jit(solution)/shard_map/all_gather | solution.py:231
  848.1 50.1 %copy-start.18 = (bf16[768,3,64]{0,2,1:T(8,128)(2,1)S(1)}, bf16[768,3,64]{0,2,1:T(8,128)(2,1)}, u32[]{:S(2)}) copy-start(bf16[768,3,64]{0,2,1:T(8,128)(2,1)} %copy.43) | copy-start | bytes 884740
  851.8 423.0 %reduce-scatter.17.cloned.1.call-start = ((), (), s32[]{:S(2)}) async-start(), calls=%async_computation.16 | async-start | bytes 7864320 | tf_op jit(solution)/shard_map/reduce_scatter | solution.py:251
  918.6 7.9 slice-start.1
  918.6 8.9 slice-start.2
  955.3 7.9 slice-start
  955.3 8.0 slice-start.1
  955.3 8.9 slice-start.2
  992.1 7.9 slice-start.1
  992.1 8.9 slice-start.2
  1028.8 7.9 slice-start.1
  1028.8 8.9 slice-start.2
  1065.5 7.9 slice-start.1
  1065.5 8.9 slice-start.2
  1102.3 7.9 slice-start.1
  1102.3 8.9 slice-start.2
  1139.0 7.9 slice-start
  1139.0 7.9 slice-start.1
  1139.0 8.9 slice-start.2
  1175.7 7.9 slice-start.1
  1175.7 8.9 slice-start.2
  1205.1 43.0 %copy-start.14 = (bf16[4096,3,64]{0,2,1:T(8,128)(2,1)}, bf16[4096,3,64]{0,2,1:T(8,128)(2,1)S(1)}, u32[]{:S(2)}) copy-start(bf16[4096,3,64]{0,2,1:T(8,128)(2,1)S(1)} %convert.10) | copy-start | bytes 4718596
  1216.0 125.5 %reduce-scatter.25.cloned.1.call-start = ((), (), s32[]{:S(2)}) async-start(), calls=%async_computation.20 | async-start | bytes 884736
  1225.7 188.9 %reduce-scatter.23.cloned.1.call-start = ((), (), s32[]{:S(2)}) async-start(), calls=%async_computation.19 | async-start | bytes 2654208 | tf_op jit(solution)/shard_map/reduce_scatter | solution.py:267
  1236.8 250.8 %reduce-scatter.21.cloned.1.call-start = ((), (), s32[]{:S(2)}) async-start(), calls=%async_computation.18 | async-start | bytes 2654208 | tf_op jit(solution)/shard_map/reduce_scatter | solution.py:266
  1247.8 312.8 %reduce-scatter.19.cloned.1.call-start = ((), (), s32[]{:S(2)}) async-start(), calls=%async_computation.17 | async-start | bytes 2654208 | tf_op jit(solution)/shard_map/reduce_scatter | solution.py:264
  1257.9 16.9 %copy-start.7 = (f32[1024,768]{1,0:T(8,128)S(1)}, f32[1024,768]{1,0:T(8,128)}, u32[]{:S(2)}) copy-start(f32[1024,768]{1,0:T(8,128)} %copy-done.6) | copy-start | bytes 9437188
  1257.9 16.9 %copy-start.26 = (f32[1024]{0:T(1024)S(1)}, f32[1024]{0:T(1024)}, u32[]{:S(2)}) copy-start(f32[1024]{0:T(1024)} %copy-done.25) | copy-start | bytes 12292
  1258.0 302.6 %all-reduce.4.cloned.1.call-start = ((), (), s32[]{:S(2)}) async-start(), calls=%async_computation.21 | async-start | bytes 196608 | tf_op jit(solution)/shard_map/psum | solution.py:278
  1260.9 17.4 %copy-start.30 = (s32[1024]{0:T(1024)S(1)}, s32[1024]{0:T(1024)}, u32[]{:S(2)}) copy-start(s32[1024]{0:T(1024)} %copy-done.29) | copy-start | bytes 12292
  1260.9 17.4 %copy-start.41 = (s32[40]{0:T(128)S(1)}, s32[40]{0:T(128)}, u32[]{:S(2)}) copy-start(s32[40]{0:T(128)} %copy-done.40) | copy-start | bytes 484
  1260.9 19.5 %copy-start.32 = (f32[768]{0:T(1024)S(1)}, f32[768]{0:T(1024)}, u32[]{:S(2)}) copy-start(f32[768]{0:T(1024)} %get-tuple-element.493) | copy-start | bytes 9220
  (71 other events, 286.4 us)
Sparse Core Ops, SparseCore 0:
  15.0 49.0 all-gather.5
  312.6 98.7 reduce-scatter.10
  742.7 99.6 reduce-scatter.14
  1280.5 133.8 all-reduce.3
Sparse Core Ops, SparseCore 1:
  315.2 40.3 all-gather.9
  418.1 46.2 all-gather.7
  466.4 41.3 all-gather.11
  518.2 98.1 reduce-scatter.12
  851.9 46.2 all-gather.13
  1216.1 58.7 reduce-scatter.16
  1278.0 63.4 reduce-scatter.24
  1345.4 69.1 reduce-scatter.22
  1418.5 69.0 reduce-scatter.20
  1491.6 68.9 reduce-scatter.18
